TPU v7x, 256 devices: a whole 4x4x8 slice. The times are simulated.
256 devices in a mesh: row: 32 (over x, z), col: 8 (over y, core).
Axes of the slice: x: 4, y: 4, z: 8, core: 2. Of those that a mesh axis runs over, the one named last changes fastest.
Arguments:
- incident: float32 [2, 36, 32768], P(None, None, 'row'), may hold values from -24 to 24
- diagonal: float32 [32768], P('row'), may hold values from 1 to 2
- near_blocks: bfloat16 [32, 8, 2, 1024, 1024], P('row', None, None, None, 'col'), may hold values from -0.046875 to 0.046875
- left_factors: bfloat16 [32, 32, 2, 64, 1024], P('row', 'col'), may hold values from -0.0390625 to 0.0390625
- right_factors: bfloat16 [32, 32, 2, 64, 1024], P('row', 'col'), may hold values from -0.1875 to 0.1875
- flags: int32 [32, 8], P('row'), may hold values from 0 to 1, as said below
- ranks: int32 [32, 32], P('row', 'col'), may hold values from 4 to 64
- harmonics: float32 [2, 36, 32768], P(None, None, 'row'), may hold values from -0.03125 to 0.03125
Outputs:
- solution: float32 [2, 36, 32768], P(None, None, 'row')
- coefficients: float32 [2, 36, 36], replicated
Inputs may be any that keep to these rules, and one draw needn't show every extreme that they name: `flags`: slot 8 / 2 (the pair of a cluster with itself) is always 1; the ones of a row form one run of slots around it.
All inputs are finite; a program needn't handle non-finite values.
Results may differ from a plain program's by a relative error of at most 0.0013.
Values may be sent and summed in bfloat16 or wider, within the bound.
A program may use at most 128 MiB of HBM per device.

v0:
```python
from functools import partial
import jax
import jax.numpy as jnp
from jax import lax
from jax.sharding import PartitionSpec as P

highest = lax.Precision.HIGHEST


def dense_term(vector, block):

    def product(left, right):
        return jnp.einsum("sf,ef->se", left, right, preferred_element_type=jnp.float32)

    real_out = product(vector[0], block[0]) - product(vector[1], block[1])
    imag_out = product(vector[0], block[1]) + product(vector[1], block[0])
    return jnp.stack([real_out, imag_out])


def lowrank_term(vector, left_block, right_block, rank):

    def inner(left, right):
        return jnp.einsum("sf,rf->sr", left, right, preferred_element_type=jnp.float32)

    def outer(left, right):
        return jnp.einsum("sr,re->se", left, right, preferred_element_type=jnp.float32)

    coeff_real = inner(vector[0], right_block[0]) - inner(vector[1], right_block[1])
    coeff_imag = inner(vector[0], right_block[1]) + inner(vector[1], right_block[0])
    keep = (jnp.arange(right_block.shape[1], dtype=jnp.int32) < rank)[None, None, :]
    coeffs = jnp.where(keep, jnp.stack([coeff_real, coeff_imag]), 0.0).astype(jnp.bfloat16)
    real_out = outer(coeffs[0], left_block[0]) - outer(coeffs[1], left_block[1])
    imag_out = outer(coeffs[0], left_block[1]) + outer(coeffs[1], left_block[0])
    return jnp.stack([real_out, imag_out])


def inner_products(first, second):
    return jnp.einsum("csn,ctn->st", first, second, precision=highest)


def combine_rows(matrix, vectors):
    return jnp.einsum("st,ctn->csn", matrix, vectors, precision=highest)


def matmul(left, right):
    return jnp.dot(left, right, precision=highest)


def lower_inverse(lower):
    identity = jnp.eye(lower.shape[0], dtype=lower.dtype)
    return lax.linalg.triangular_solve(lower, identity, left_side=True, lower=True)


def project(harmonics, vectors):

    def contract(left, right):
        return jnp.einsum("mn,sn->ms", left, right, precision=highest)

    real_out = contract(harmonics[0], vectors[0]) + contract(harmonics[1], vectors[1])
    imag_out = contract(harmonics[0], vectors[1]) - contract(harmonics[1], vectors[0])
    return jnp.stack([real_out, imag_out])


def body(incident, diagonal, near_blocks, left_factors, right_factors, flags, ranks, harmonics):
    blocks = left_factors.shape[1]
    slots = near_blocks.shape[1]
    width = near_blocks.shape[4]
    half_band = slots // 2
    elements = incident.shape[2]
    fields = incident.shape[1]
    clusters = lax.axis_size("row")
    row_index = lax.axis_index("row")
    column = lax.axis_index("col")
    empty = jnp.zeros((2, fields, elements), jnp.float32)

    def far_term(number, piece):
        cluster = column * blocks + number
        offset = (cluster - row_index + half_band) % clusters
        is_near = (offset < slots) & (flags[0, jnp.minimum(offset, slots - 1)] == 1)
        return lax.cond(
            is_near,
            lambda operand: empty,
            partial(
                lowrank_term,
                left_block=left_factors[0, number],
                right_block=right_factors[0, number],
                rank=ranks[0, number],
            ),
            piece,
        )

    def near_term(slot, piece):
        return lax.cond(
            flags[0, slot] == 1,
            partial(dense_term, block=near_blocks[0, slot]),
            lambda operand: empty,
            piece,
        )

    def apply_operator(vector):
        rounded = vector.astype(jnp.bfloat16)
        gathered = lax.all_gather(rounded, "row", axis=2, tiled=True)
        far_pieces = [
            lax.dynamic_slice_in_dim(gathered, (column * blocks + number) * elements, elements, 2)
            for number in range(blocks)
        ]
        near_pieces = [
            lax.dynamic_slice_in_dim(
                gathered,
                (row_index + slot - half_band) % clusters * elements + column * width,
                width,
                2,
            )
            for slot in range(slots)
        ]
        total = near_term(0, near_pieces[0])
        for slot in range(1, slots):
            total = total + near_term(slot, near_pieces[slot])
        for number in range(blocks):
            total = total + far_term(number, far_pieces[number])
        summed = lax.psum(total, "col")
        return summed + diagonal[None, None, :] * vector

    lower_first = jnp.linalg.cholesky(lax.psum(inner_products(incident, incident), "row"))
    basis_one = combine_rows(lower_inverse(lower_first), incident)
    image = apply_operator(basis_one)
    coupling_one = lax.psum(inner_products(image, basis_one), "row")
    rest = image - combine_rows(coupling_one, basis_one)
    gram_one = lax.psum(inner_products(rest, rest), "row")
    lower_second = jnp.linalg.cholesky(gram_one)
    basis_two = combine_rows(lower_inverse(lower_second), rest)
    image = apply_operator(basis_two)
    coupling_onetwo, coupling_two = lax.psum(
        (inner_products(image, basis_one), inner_products(image, basis_two)), "row"
    )
    rest = image - combine_rows(coupling_onetwo, basis_one) - combine_rows(coupling_two, basis_two)
    gram_two = lax.psum(inner_products(rest, rest), "row")
    upper_left = matmul(coupling_one, coupling_one.T) + gram_one
    upper_right = matmul(coupling_one, coupling_onetwo.T) + matmul(lower_second, coupling_two.T)
    lower_right = (
        matmul(coupling_onetwo, coupling_onetwo.T) + matmul(coupling_two, coupling_two.T) + gram_two
    )
    normal = jnp.concatenate(
        [
            jnp.concatenate([upper_left, upper_right], axis=1),
            jnp.concatenate([upper_right.T, lower_right], axis=1),
        ],
        axis=0,
    )
    target = jnp.concatenate(
        [matmul(lower_first, coupling_one.T), matmul(lower_first, coupling_onetwo.T)], axis=1
    )
    factor_inverse = lower_inverse(jnp.linalg.cholesky(normal))
    weights = matmul(factor_inverse.T, matmul(factor_inverse, target.T)).T
    first_weights = weights[:, :fields]
    second_weights = weights[:, fields:]
    solution = combine_rows(first_weights, basis_one) + combine_rows(second_weights, basis_two)
    coefficients = lax.psum(project(harmonics, solution), "row")
    return (solution, coefficients)


def solution(mesh):
    in_specs = (
        P(None, None, "row"),
        P("row"),
        P("row", None, None, None, "col"),
        P("row", "col", None, None, None),
        P("row", "col", None, None, None),
        P("row", None),
        P("row", "col"),
        P(None, None, "row"),
    )
    out_specs = (P(None, None, "row"), P())
    return jax.shard_map(body, mesh=mesh, in_specs=in_specs, out_specs=out_specs, check_vma=False)
```

profile of v0, /device:TPU:0, one launch (start us, length us, event | category | flops | bytes accessed | tf_op | source)
XLA Modules:
  0.0 1355.9 jit_solution(15684794761179191939)
XLA Ops:
  8.8 144.0 %psum.63 = f32[36,36]{0,1:T(8,128)S(1)} all-reduce(f32[36,36]{0,1:T(8,128)S(1)} %convolution_bitcast_fusion.12), channel_id=1, replica_groups=mesh['row'=32,'col'=8] {'row'}, use_global_device_ids=true, to_apply=%region_0.0 | all-reduce | flops 1296 | bytes 10368 | tf_op jit(solution)/shard_map/psum | solution.py:124
  152.9 3.3 cholesky.81
  173.7 2.8 slice_bitcast_fusion.62
  178.0 64.0 %all-gather.3.cloned.1.call-done = bf16[2,36,32768]{2,1,0:T(8,128)(2,1)} async-done(((bf16[2,36,1024]{2,1,0:T(8,128)(2,1)}), bf16[2,36,32768]{2,1,0:T(8,128)(2,1)}) %all-gather.3.cloned.1.call-update) | async-done | bytes 4718608 | tf_op jit(solution)/shard_map/all_gather | solution.py:102
  245.0 6.4 conditional.31
  251.5 6.4 conditional.30
  257.9 4.9 conditional.29
  262.8 4.9 conditional.28
  267.7 4.8 conditional.27
  272.5 4.8 conditional.26
  277.3 4.8 conditional.24
  282.1 4.8 conditional.25
  286.9 3.0 add_add_fusion.1
  290.0 99.7 %all-reduce.4.cloned.1.call-done = f32[2,36,1024]{2,1,0:T(8,128)} async-done(((f32[2,36,1024]{2,1,0:T(8,128)}), f32[2,36,1024]{2,1,0:T(8,128)}) %all-reduce.4.cloned.1.call-update) | async-done | bytes 294928 | tf_op jit(solution)/shard_map/psum | solution.py:121
  391.1 143.1 %psum.65 = f32[36,36]{1,0:T(8,128)S(1)} all-reduce(f32[36,36]{1,0:T(8,128)S(1)} %convolution_bitcast_fusion.10), channel_id=1, replica_groups=mesh['row'=32,'col'=8] {'row'}, use_global_device_ids=true, to_apply=%region_28.31 | all-reduce | flops 1296 | bytes 10368 | tf_op jit(solution)/shard_map/psum | solution.py:127
  536.7 137.9 %psum.66 = f32[36,36]{1,0:T(8,128)S(1)} all-reduce(f32[36,36]{1,0:T(8,128)S(1)} %convolution_bitcast_fusion.9), channel_id=1, replica_groups=mesh['row'=32,'col'=8] {'row'}, use_global_device_ids=true, to_apply=%region_29.32 | all-reduce | flops 1296 | bytes 10368 | tf_op jit(solution)/shard_map/psum | solution.py:129
  674.8 3.3 cholesky.92
  687.5 73.5 %all-gather.5.cloned.1.call-done = bf16[2,36,32768]{2,1,0:T(8,128)(2,1)} async-done(((bf16[2,36,1024]{2,1,0:T(8,128)(2,1)}), bf16[2,36,32768]{2,1,0:T(8,128)(2,1)}) %all-gather.5.cloned.1.call-update) | async-done | bytes 4718608 | tf_op jit(solution)/shard_map/all_gather | solution.py:102
  764.1 5.7 conditional.43
  769.9 5.7 conditional.42
  775.6 5.7 conditional.41
  781.3 4.0 conditional.40
  786.1 4.8 conditional.39
  790.8 4.9 conditional.38
  795.7 4.1 conditional.36
  799.8 4.1 conditional.37
  807.4 97.7 %all-reduce.6.cloned.1.call-done = f32[2,36,1024]{2,1,0:T(8,128)} async-done(((f32[2,36,1024]{2,1,0:T(8,128)}), f32[2,36,1024]{2,1,0:T(8,128)}) %all-reduce.6.cloned.1.call-update) | async-done | bytes 294928 | tf_op jit(solution)/shard_map/psum | solution.py:121
  907.8 143.1 %all-reduce = (f32[36,36]{1,0:T(8,128)S(1)}, f32[36,36]{1,0:T(8,128)S(1)}) all-reduce(f32[36,36]{1,0:T(8,128)S(1)} %convolution_bitcast_fusion.7, f32[36,36]{1,0:T(8,128)S(1)} %convolution_bitcast_fusion.6), channel_id=1, replica_groups=mesh['row'=32,'col'=8] {'row'}, use_global_device_ids=true, to_apply=%region_55.58 | all-reduce | flops 2592 | bytes 20736 | tf_op jit(solution)/shard_map/psum | solution.py:133
  1054.4 137.9 %psum.70 = f32[36,36]{0,1:T(8,128)S(1)} all-reduce(f32[36,36]{0,1:T(8,128)S(1)} %convolution_bitcast_fusion.5), channel_id=1, replica_groups=mesh['row'=32,'col'=8] {'row'}, use_global_device_ids=true, to_apply=%region_57.60 | all-reduce | flops 1296 | bytes 10368 | tf_op jit(solution)/shard_map/psum | solution.py:137
  1193.7 6.6 cholesky.42
  1201.6 5.5 custom-call.11
  1210.9 137.7 %psum.71 = f32[2,36,36]{1,2,0:T(8,128)S(1)} all-reduce(f32[2,36,36]{1,2,0:T(8,128)S(1)} %pad_maximum_fusion.24), channel_id=1, replica_groups=mesh['row'=32,'col'=8] {'row'}, use_global_device_ids=true, to_apply=%region_60.63 | all-reduce | flops 2592 | bytes 20736 | tf_op jit(solution)/shard_map/psum | solution.py:158
  (204 shorter events, 136.7 us)
Async XLA Ops:
  7.2 234.8 %all-gather.3.cloned.1.call-start = ((), (), s32[]{:S(2)}) async-start(), calls=%async_computation | async-start | bytes 5406720 | tf_op jit(solution)/shard_map/all_gather | solution.py:102
  156.2 4.1 copy-start.15
  162.7 227.0 %all-reduce.4.cloned.1.call-start = ((), (), s32[]{:S(2)}) async-start(), calls=%async_computation.1 | async-start | bytes 655360 | tf_op jit(solution)/shard_map/psum | solution.py:121
  172.2 4.4 copy-start.3
  178.0 79.9 %copy-start = (bf16[2,1024,128]{2,1,0:T(8,128)(2,1)}, bf16[2,1024,128]{2,1,0:T(8,128)(2,1)S(1)}, u32[]{:S(2)}) copy-start(bf16[2,1024,128]{2,1,0:T(8,128)(2,1)S(1)} %get-tuple-element.571) | copy-start | bytes 1572868
  262.8 4.9 copy-start.10
  272.5 14.4 %copy-start.6 = (f32[2,36,1024]{2,1,0:T(8,128)S(1)}, f32[2,36,1024]{2,1,0:T(8,128)}, u32[]{:S(2)}) copy-start(f32[2,36,1024]{2,1,0:T(8,128)} %get-tuple-element.623) | copy-start | bytes 884740
  277.3 112.4 %copy-start.19 = (f32[1024]{0:T(1024)S(1)}, f32[1024]{0:T(1024)}, u32[]{:S(2)}) copy-start(f32[1024]{0:T(1024)} %param.60) | copy-start | bytes 12292
  290.0 471.1 %all-gather.5.cloned.1.call-start = ((), (), s32[]{:S(2)}) async-start(), calls=%async_computation.2 | async-start | bytes 5406720 | tf_op jit(solution)/shard_map/all_gather | solution.py:102
  534.2 226.9 %copy-start.13 = (f32[36,36]{1,0:T(8,128)}, f32[36,36]{1,0:T(8,128)S(1)}, u32[]{:S(2)}) copy-start(f32[36,36]{1,0:T(8,128)S(1)} %psum.65) | copy-start | bytes 15556
  535.6 0.7 copy-start.2
  678.1 4.1 copy-start.17
  684.5 220.5 %all-reduce.6.cloned.1.call-start = ((), (), s32[]{:S(2)}) async-start(), calls=%async_computation.3 | async-start | bytes 655360 | tf_op jit(solution)/shard_map/psum | solution.py:121
  761.1 2.3 copy-start.1
  785.4 0.7 copy-start.11
  790.8 13.1 copy-start.7
  790.8 13.1 copy-start.8
  790.8 13.1 copy-start.9
  795.7 8.2 copy-start.12
  795.7 10.8 copy-start.14
  795.7 10.8 copy-start.16
  803.9 388.4 %copy-start.18 = (f32[36,36]{1,0:T(8,128)S(1)}, f32[36,36]{1,0:T(8,128)}, u32[]{:S(2)}) copy-start(f32[36,36]{1,0:T(8,128)} %copy-done.17) | copy-start | bytes 15556
  803.9 389.2 %copy-start.20 = (f32[36,36]{1,0:T(8,128)S(1)}, f32[36,36]{1,0:T(8,128)}, u32[]{:S(2)}) copy-start(f32[36,36]{1,0:T(8,128)} %convolution_add_fusion.36) | copy-start | bytes 15556
  806.5 403.3 %copy-start.5 = (f32[1,36,1024]{2,0,1:T(1,128)S(1)}, f32[1,36,1024]{2,0,1:T(1,128)}, u32[]{:S(2)}) copy-start(f32[1,36,1024]{2,0,1:T(1,128)} %get-tuple-element.587) | copy-start | bytes 442372
  806.5 403.9 %copy-start.4 = (f32[1,36,1024]{2,0,1:T(1,128)S(1)}, f32[1,36,1024]{2,0,1:T(1,128)}, u32[]{:S(2)}) copy-start(f32[1,36,1024]{2,0,1:T(1,128)} %get-tuple-element.586) | copy-start | bytes 442372
Sparse Core Ops, SparseCore 0:
  162.8 79.1 all-gather.2
  290.1 99.5 all-reduce.3
  684.7 76.3 all-gather.4
  806.6 98.3 all-reduce.5
where the time goes:
time: 1360 us
  blocking collectives  844 us (62%)
  waiting for transfers between devices  335 us (25%)
  matrix products  92.1 us (7%)
  other arithmetic  43.3 us (3%)
  between operations  21.8 us (2%)
  local copies, waits for them, and re-layouts  19.4 us (1%)
    psum x2, waiting for transfers between devices, apply_operator(): summed = lax.psum(total, 'col')  197 us
    psum x1, blocking collectives, body(): lax.psum(inner_products(incident, incident), 'row')  144 us
    psum x1, blocking collectives, body(): lax.psum((inner_products(image, basis_one), inner_products(image, basis_t...  143 us
    psum x1, blocking collectives, body(): coupling_one = lax.psum(inner_products(image, basis_one), 'row')  143 us
    psum x1, blocking collectives, body(): gram_two = lax.psum(inner_products(rest, rest), 'row')  138 us
    psum x1, blocking collectives, body(): gram_one = lax.psum(inner_products(rest, rest), 'row')  138 us
    psum x1, blocking collectives, body(): coefficients = lax.psum(project(harmonics, solution), 'row')  138 us
    all_gather x2, waiting for transfers between devices, apply_operator(): gathered = lax.all_gather(rounded, 'row', axis=2, tiled=True)  138 us
  transfers between devices with their start and end apart: 4, of which 4 were waited for; matrix products, arithmetic and copies ran while one was open for 1% of the time, Pallas kernels for 0%

commit v1 on v0

--- a/solution.py
+++ b/solution.py
@@ -155,7 +155,7 @@
     first_weights = weights[:, :fields]
     second_weights = weights[:, fields:]
     solution = combine_rows(first_weights, basis_one) + combine_rows(second_weights, basis_two)
-    coefficients = lax.psum(project(harmonics, solution), "row")
+    coefficients = jnp.sum(lax.all_gather(project(harmonics, solution), "row"), axis=0)
     return (solution, coefficients)
 
 

time: 1360 us -> 1270 us (0.934)
  blocking collectives: 844 us -> 753 us
    psum x1 -> x0, blocking collectives: 138 us -> none  [body(): coefficients = lax.psum(project(harmonics, solution), 'row')]
    all_gather x0 -> x1, blocking collectives: none -> 46.9 us  [body(): lax.all_gather(project(harmonics, solution), 'row')]
where the time goes in v1:
time: 1270 us
  blocking collectives  753 us (59%)
  waiting for transfers between devices  335 us (26%)
  matrix products  92 us (7%)
  other arithmetic  43.5 us (3%)
  between operations  21.8 us (2%)
  local copies, waits for them, and re-layouts  19.5 us (2%)
    psum x2, waiting for transfers between devices, apply_operator(): summed = lax.psum(total, 'col')  197 us
    psum x1, blocking collectives, body(): lax.psum(inner_products(incident, incident), 'row')  144 us
    psum x1, blocking collectives, body(): lax.psum((inner_products(image, basis_one), inner_products(image, basis_t...  143 us
    psum x1, blocking collectives, body(): coupling_one = lax.psum(inner_products(image, basis_one), 'row')  143 us
    psum x1, blocking collectives, body(): gram_two = lax.psum(inner_products(rest, rest), 'row')  138 us
    psum x1, blocking collectives, body(): gram_one = lax.psum(inner_products(rest, rest), 'row')  138 us
    all_gather x2, waiting for transfers between devices, apply_operator(): gathered = lax.all_gather(rounded, 'row', axis=2, tiled=True)  138 us
    dot_general x64, matrix products, product(): jnp.einsum('sf,ef->se', left, right, preferred_element_type=jnp.float32)  71.2 us
  transfers between devices with their start and end apart: 4, of which 4 were waited for; matrix products, arithmetic and copies ran while one was open for 1% of the time, Pallas kernels for 0%

profile of v1, /device:TPU:0, one launch (start us, length us, event | category | flops | bytes accessed | tf_op | source)
XLA Modules:
  0.0 1265.2 jit_solution(13109600922273202475)
XLA Ops:
  8.8 144.0 %psum.56 = f32[36,36]{0,1:T(8,128)S(1)} all-reduce(f32[36,36]{0,1:T(8,128)S(1)} %convolution_bitcast_fusion.12), channel_id=1, replica_groups=mesh['row'=32,'col'=8] {'row'}, use_global_device_ids=true, to_apply=%region_0.0 | all-reduce | flops 1296 | bytes 10368 | tf_op jit(solution)/shard_map/psum | solution.py:124
  152.9 3.3 cholesky.81
  173.7 2.8 slice_bitcast_fusion.62
  178.0 64.0 %all-gather.4.cloned.1.call-done = bf16[2,36,32768]{2,1,0:T(8,128)(2,1)} async-done(((bf16[2,36,1024]{2,1,0:T(8,128)(2,1)}), bf16[2,36,32768]{2,1,0:T(8,128)(2,1)}) %all-gather.4.cloned.1.call-update) | async-done | bytes 4718608 | tf_op jit(solution)/shard_map/all_gather | solution.py:102
  245.0 6.4 conditional.31
  251.5 6.4 conditional.30
  257.9 4.9 conditional.29
  262.8 4.9 conditional.28
  267.7 4.8 conditional.27
  272.5 4.8 conditional.26
  277.3 4.8 conditional.24
  282.1 4.8 conditional.25
  286.9 3.0 add_add_fusion.1
  290.0 99.7 %all-reduce.4.cloned.1.call-done = f32[2,36,1024]{2,1,0:T(8,128)} async-done(((f32[2,36,1024]{2,1,0:T(8,128)}), f32[2,36,1024]{2,1,0:T(8,128)}) %all-reduce.4.cloned.1.call-update) | async-done | bytes 294928 | tf_op jit(solution)/shard_map/psum | solution.py:121
  391.1 143.1 %psum.58 = f32[36,36]{1,0:T(8,128)S(1)} all-reduce(f32[36,36]{1,0:T(8,128)S(1)} %convolution_bitcast_fusion.10), channel_id=1, replica_groups=mesh['row'=32,'col'=8] {'row'}, use_global_device_ids=true, to_apply=%region_28.31 | all-reduce | flops 1296 | bytes 10368 | tf_op jit(solution)/shard_map/psum | solution.py:127
  536.7 137.9 %psum.59 = f32[36,36]{1,0:T(8,128)S(1)} all-reduce(f32[36,36]{1,0:T(8,128)S(1)} %convolution_bitcast_fusion.9), channel_id=1, replica_groups=mesh['row'=32,'col'=8] {'row'}, use_global_device_ids=true, to_apply=%region_29.32 | all-reduce | flops 1296 | bytes 10368 | tf_op jit(solution)/shard_map/psum | solution.py:129
  674.8 3.3 cholesky.92
  687.5 73.5 %all-gather.6.cloned.1.call-done = bf16[2,36,32768]{2,1,0:T(8,128)(2,1)} async-done(((bf16[2,36,1024]{2,1,0:T(8,128)(2,1)}), bf16[2,36,32768]{2,1,0:T(8,128)(2,1)}) %all-gather.6.cloned.1.call-update) | async-done | bytes 4718608 | tf_op jit(solution)/shard_map/all_gather | solution.py:102
  764.1 5.7 conditional.43
  769.9 5.7 conditional.42
  775.6 5.7 conditional.41
  781.3 4.0 conditional.40
  786.1 4.8 conditional.39
  790.8 4.9 conditional.38
  795.7 4.1 conditional.36
  799.8 4.1 conditional.37
  807.4 97.7 %all-reduce.6.cloned.1.call-done = f32[2,36,1024]{2,1,0:T(8,128)} async-done(((f32[2,36,1024]{2,1,0:T(8,128)}), f32[2,36,1024]{2,1,0:T(8,128)}) %all-reduce.6.cloned.1.call-update) | async-done | bytes 294928 | tf_op jit(solution)/shard_map/psum | solution.py:121
  907.8 143.1 %all-reduce = (f32[36,36]{1,0:T(8,128)S(1)}, f32[36,36]{1,0:T(8,128)S(1)}) all-reduce(f32[36,36]{1,0:T(8,128)S(1)} %convolution_bitcast_fusion.7, f32[36,36]{1,0:T(8,128)S(1)} %convolution_bitcast_fusion.6), channel_id=1, replica_groups=mesh['row'=32,'col'=8] {'row'}, use_global_device_ids=true, to_apply=%region_55.58 | all-reduce | flops 2592 | bytes 20736 | tf_op jit(solution)/shard_map/psum | solution.py:133
  1054.4 138.0 %psum.63 = f32[36,36]{0,1:T(8,128)S(1)} all-reduce(f32[36,36]{0,1:T(8,128)S(1)} %convolution_bitcast_fusion.5), channel_id=1, replica_groups=mesh['row'=32,'col'=8] {'row'}, use_global_device_ids=true, to_apply=%region_57.60 | all-reduce | flops 1296 | bytes 10368 | tf_op jit(solution)/shard_map/psum | solution.py:137
  1193.8 6.6 cholesky.42
  1201.7 5.5 custom-call.11
  1211.0 46.9 %all-gather = f32[64,36,36]{2,1,0:T(8,128)S(1)} all-gather(f32[2,36,36]{2,1,0:T(8,128)S(1)} %copy.52), channel_id=2, replica_groups=mesh['row'=32,'col'=8] {'row'}, dimensions={0}, use_global_device_ids=true | all-gather | bytes 342144 | tf_op jit(solution)/shard_map/all_gather | solution.py:158
  (206 shorter events, 136.7 us)
Async XLA Ops:
  7.2 234.8 %all-gather.4.cloned.1.call-start = ((), (), s32[]{:S(2)}) async-start(), calls=%async_computation | async-start | bytes 5406720 | tf_op jit(solution)/shard_map/all_gather | solution.py:102
  156.2 4.1 copy-start.15
  162.7 227.0 %all-reduce.4.cloned.1.call-start = ((), (), s32[]{:S(2)}) async-start(), calls=%async_computation.1 | async-start | bytes 655360 | tf_op jit(solution)/shard_map/psum | solution.py:121
  172.2 4.4 copy-start.3
  178.0 79.9 %copy-start = (bf16[2,1024,128]{2,1,0:T(8,128)(2,1)}, bf16[2,1024,128]{2,1,0:T(8,128)(2,1)S(1)}, u32[]{:S(2)}) copy-start(bf16[2,1024,128]{2,1,0:T(8,128)(2,1)S(1)} %get-tuple-element.573) | copy-start | bytes 1572868
  262.8 4.9 copy-start.10
  272.5 14.4 %copy-start.6 = (f32[2,36,1024]{2,1,0:T(8,128)S(1)}, f32[2,36,1024]{2,1,0:T(8,128)}, u32[]{:S(2)}) copy-start(f32[2,36,1024]{2,1,0:T(8,128)} %get-tuple-element.625) | copy-start | bytes 884740
  277.3 112.4 %copy-start.19 = (f32[1024]{0:T(1024)S(1)}, f32[1024]{0:T(1024)}, u32[]{:S(2)}) copy-start(f32[1024]{0:T(1024)} %param.60) | copy-start | bytes 12292
  290.0 471.1 %all-gather.6.cloned.1.call-start = ((), (), s32[]{:S(2)}) async-start(), calls=%async_computation.2 | async-start | bytes 5406720 | tf_op jit(solution)/shard_map/all_gather | solution.py:102
  534.2 226.9 %copy-start.13 = (f32[36,36]{1,0:T(8,128)}, f32[36,36]{1,0:T(8,128)S(1)}, u32[]{:S(2)}) copy-start(f32[36,36]{1,0:T(8,128)S(1)} %psum.58) | copy-start | bytes 15556
  535.6 0.7 copy-start.2
  678.1 4.1 copy-start.17
  684.5 220.5 %all-reduce.6.cloned.1.call-start = ((), (), s32[]{:S(2)}) async-start(), calls=%async_computation.3 | async-start | bytes 655360 | tf_op jit(solution)/shard_map/psum | solution.py:121
  761.1 2.3 copy-start.1
  785.4 0.7 copy-start.11
  790.8 13.1 %copy-start.7 = (f32[2,36,1024]{2,1,0:T(8,128)S(1)}, f32[2,36,1024]{2,1,0:T(8,128)}, u32[]{:S(2)}) copy-start(f32[2,36,1024]{2,1,0:T(8,128)} %get-tuple-element.637) | copy-start | bytes 884740
  790.8 13.1 %copy-start.8 = (f32[2,36,1024]{2,1,0:T(8,128)S(1)}, f32[2,36,1024]{2,1,0:T(8,128)}, u32[]{:S(2)}) copy-start(f32[2,36,1024]{2,1,0:T(8,128)} %get-tuple-element.636) | copy-start | bytes 884740
  790.8 13.1 %copy-start.9 = (f32[2,36,1024]{2,1,0:T(8,128)S(1)}, f32[2,36,1024]{2,1,0:T(8,128)}, u32[]{:S(2)}) copy-start(f32[2,36,1024]{2,1,0:T(8,128)} %get-tuple-element.635) | copy-start | bytes 884740
  795.7 8.2 copy-start.12
  795.7 10.8 copy-start.14
  795.7 10.8 copy-start.16
  803.9 388.5 %copy-start.18 = (f32[36,36]{1,0:T(8,128)S(1)}, f32[36,36]{1,0:T(8,128)}, u32[]{:S(2)}) copy-start(f32[36,36]{1,0:T(8,128)} %copy-done.17) | copy-start | bytes 15556
  803.9 389.3 %copy-start.20 = (f32[36,36]{1,0:T(8,128)S(1)}, f32[36,36]{1,0:T(8,128)}, u32[]{:S(2)}) copy-start(f32[36,36]{1,0:T(8,128)} %convolution_add_fusion.36) | copy-start | bytes 15556
  806.5 403.3 %copy-start.5 = (f32[1,36,1024]{2,0,1:T(1,128)S(1)}, f32[1,36,1024]{2,0,1:T(1,128)}, u32[]{:S(2)}) copy-start(f32[1,36,1024]{2,0,1:T(1,128)} %get-tuple-element.589) | copy-start | bytes 442372
  806.5 403.8 %copy-start.4 = (f32[1,36,1024]{2,0,1:T(1,128)S(1)}, f32[1,36,1024]{2,0,1:T(1,128)}, u32[]{:S(2)}) copy-start(f32[1,36,1024]{2,0,1:T(1,128)} %get-tuple-element.588) | copy-start | bytes 442372
Sparse Core Ops, SparseCore 0:
  162.8 79.1 all-gather.3
  290.1 99.5 all-reduce.3
  684.7 76.3 all-gather.5
  806.6 98.3 all-reduce.5
